TPU v7x, 512 devices: a whole 4x4x16 slice. The times are simulated.
512 devices in a mesh: view: 32 (over y_lo, z), band: 4 (over x), batch: 4 (over y_hi, core).
Axes of the slice: x: 4, y: 4 (y_hi: 2, y_lo: 2; y = y_hi * 2 + y_lo), z: 16, core: 2. Of those that a mesh axis runs over, the one named last changes fastest.
Arguments:
- images: bfloat16 [128, 32, 16, 768], P(('batch', 'view'), 'band'), parts along dimension 0, may hold values from -6 to 6
- frame_gain: float32 [768], replicated, may hold values from 0.5 to 2.5
- frame_qkv: bfloat16 [768, 1536], replicated, may hold values from -0.3 to 0.3
- frame_out: bfloat16 [512, 768], replicated, may hold values from -0.25 to 0.25
- row1_gain: float32 [768], replicated, may hold values from 0.5 to 2.5
- row1_qkv: bfloat16 [768, 1536], P('band'), may hold values from -0.3 to 0.3
- row1_out: bfloat16 [512, 768], P(None, 'band'), may hold values from -0.25 to 0.25
- row2_gain: float32 [768], replicated, may hold values from 0.5 to 2.5
- row2_qkv: bfloat16 [768, 1536], P('band'), may hold values from -0.3 to 0.3
- row2_out: bfloat16 [512, 768], P(None, 'band'), may hold values from -0.25 to 0.25
Outputs:
- refined: bfloat16 [128, 32, 16, 768], P(('batch', 'view'), 'band'), parts along dimension 0
There are 4 independent parts, one for each index of `batch`. A program takes and returns all parts, laid end to end along the dimension named above; an argument that names none is the same for every part. Nothing has to cross between parts.
All inputs are finite; a program needn't handle non-finite values.
Results may differ from a plain program's by a relative error of at most 0.02.
Values may be sent and summed in bfloat16 or wider, within the bound.
No kernel may reach another device: no remote copies, remote signals or barrier semaphores. Data moves between devices by JAX's collectives and lax.ppermute only.
A program may use at most 64 MiB of HBM per device.

v0:
```python
import jax
import jax.numpy as jnp
from jax import lax
from jax.sharding import PartitionSpec as P

HEAD_DIM = 64
EPSILON = 1e-06
BLOCK_ROWS = 512


def rms_normed(stream, gain):
    values = stream.astype(jnp.float32)
    factor = lax.rsqrt(jnp.mean(values * values, axis=-1, keepdims=True) + EPSILON)
    return (values * factor * gain).astype(jnp.bfloat16)


def online_update(carry, queries, keys, values):
    running, total, accum = carry
    scores = jnp.einsum(
        "qhd,khd->hqk", queries, keys, preferred_element_type=jnp.float32
    ) * HEAD_DIM ** (-0.5)
    highest = jnp.maximum(running, jnp.max(scores, axis=-1))
    weights = jnp.exp(scores - highest[:, :, None])
    total = jnp.sum(weights, axis=-1)
    mixed = jnp.einsum(
        "hqk,khd->qhd", weights.astype(jnp.bfloat16), values, preferred_element_type=jnp.float32
    )
    accum = mixed
    return (highest, total, accum)


def unit_attention(trio):
    queries, keys, values = trio
    length, pair_width = queries.shape
    block = min(BLOCK_ROWS, length)
    keys = keys.reshape(length, 2, HEAD_DIM)
    values = values.reshape(length, 2, HEAD_DIM)
    blocks = queries.reshape(length // block, block, 2, HEAD_DIM)

    def one_block(query_block):
        scores = jnp.einsum(
            "qhd,khd->hqk", query_block, keys, preferred_element_type=jnp.float32
        ) * HEAD_DIM ** (-0.5)
        weights = jnp.exp(scores - jnp.max(scores, axis=-1, keepdims=True))
        mixed = jnp.einsum(
            "hqk,khd->qhd", weights.astype(jnp.bfloat16), values, preferred_element_type=jnp.float32
        )
        total = jnp.transpose(jnp.sum(weights, axis=-1))
        return (mixed / total[:, :, None]).astype(jnp.bfloat16).reshape(block, pair_width)

    return lax.map(one_block, blocks).reshape(length, pair_width)


def attend_units(pieces):
    queries, keys, values = pieces
    attended = lax.map(unit_attention, (queries[0], keys[0], values[0]))
    return lax.all_to_all(attended[None], "view", split_axis=2, concat_axis=0, tiled=True)


def project_parts(normed, shard):
    groups = shard.shape[1] // (2 * HEAD_DIM)
    piece = lax.all_gather(shard, "band", axis=0, tiled=True)
    count = piece.shape[0]
    return jnp.einsum(
        "rcd,dpw->rpcw",
        normed,
        piece.reshape(count, groups, 2 * HEAD_DIM),
        preferred_element_type=jnp.float32,
    )


def mix_parts(merged, shard):
    groups = merged.shape[1]
    piece = lax.all_gather(shard, "band", axis=1, tiled=True)
    count = piece.shape[1]
    return jnp.einsum(
        "rpcw,pwn->rcn",
        merged,
        piece.reshape(groups, 2 * HEAD_DIM, count),
        preferred_element_type=jnp.float32,
    )


def row_sublayer(stream, row_count, col_count, gain, project, mix):
    width = stream.shape[1]
    normed = rms_normed(stream, gain).reshape(row_count, col_count, width)
    projected = project(normed)
    groups = projected.shape[1] // 3
    views = lax.axis_size("view")

    def unit_layout(section):
        return section.astype(jnp.bfloat16).reshape(
            views, row_count * groups // views, col_count, 2 * HEAD_DIM
        )

    triple = (
        unit_layout(projected[:, :groups]),
        unit_layout(projected[:, groups : 2 * groups]),
        unit_layout(projected[:, 2 * groups :]),
    )
    returned = attend_units(
        (
            lax.all_to_all(triple[0], "view", split_axis=0, concat_axis=2, tiled=True),
            lax.all_to_all(triple[1], "view", split_axis=0, concat_axis=2, tiled=True),
            lax.all_to_all(triple[2], "view", split_axis=0, concat_axis=2, tiled=True),
        )
    )
    merged = returned.reshape(row_count, groups, col_count, 2 * HEAD_DIM)
    update = mix(merged).reshape(row_count * col_count, width)
    return (stream.astype(jnp.float32) + update).astype(jnp.bfloat16)


def local(
    images,
    frame_gain,
    frame_qkv,
    frame_out,
    row1_gain,
    row1_qkv,
    row1_out,
    row2_gain,
    row2_qkv,
    row2_out,
):
    _, row_count, col_count, width = images.shape
    inner = frame_out.shape[0]
    heads = inner // HEAD_DIM
    tokens = row_count * col_count
    stream = images.reshape(tokens, width)
    normed = rms_normed(stream, frame_gain)
    start_state = (
        jnp.full((heads, tokens), -1e30, jnp.float32),
        jnp.zeros((heads, tokens), jnp.float32),
        jnp.zeros((tokens, heads, HEAD_DIM), jnp.float32),
    )
    triple = jnp.dot(normed, frame_qkv, preferred_element_type=jnp.float32).astype(jnp.bfloat16)
    queries = triple[:, :inner].reshape(tokens, heads, HEAD_DIM)
    keys = lax.all_gather(triple[:, inner : 2 * inner], "band", axis=0, tiled=True)
    values = lax.all_gather(triple[:, 2 * inner :], "band", axis=0, tiled=True)
    count = keys.shape[0]
    result = online_update(
        start_state,
        queries,
        keys.reshape(count, heads, HEAD_DIM),
        values.reshape(count, heads, HEAD_DIM),
    )
    _, total, accum = result
    attended = (
        (accum / jnp.transpose(total)[:, :, None]).astype(jnp.bfloat16).reshape(tokens, inner)
    )
    update = jnp.dot(attended, frame_out, preferred_element_type=jnp.float32)
    stream = (stream.astype(jnp.float32) + update).astype(jnp.bfloat16)
    stream = row_sublayer(
        stream,
        row_count,
        col_count,
        row1_gain,
        lambda normed_rows: project_parts(normed_rows, row1_qkv),
        lambda merged: mix_parts(merged, row1_out),
    )
    stream = row_sublayer(
        stream,
        row_count,
        col_count,
        row2_gain,
        lambda normed_rows: project_parts(normed_rows, row2_qkv),
        lambda merged: mix_parts(merged, row2_out),
    )
    return stream.reshape(images.shape)


def solution(mesh):
    in_specs = (
        P(("batch", "view"), "band", None, None),
        P(),
        P(),
        P(),
        P(),
        P("band", None),
        P(None, "band"),
        P(),
        P("band", None),
        P(None, "band"),
    )
    out_specs = P(("batch", "view"), "band", None, None)
    return jax.shard_map(local, mesh=mesh, in_specs=in_specs, out_specs=out_specs, check_vma=False)
```

profile of v0, /device:TPU:8, one launch (start us, length us, event | category | flops | bytes accessed | tf_op | source)
XLA Modules:
  0.0 268.4 jit_solution(17750390809118338394)
XLA Ops:
  8.0 1.0 multiply_reduce_fusion.5
  9.1 1.0 fusion.31
  11.4 13.1 %all_gather.19 = bf16[512,512]{1,0:T(8,128)(2,1)S(1)} all-gather(bf16[128,512]{1,0:T(8,128)(2,1)S(1)} %get-tuple-element.74), channel_id=1, replica_groups=mesh['view'=32,'band'=4,'batch'=4] {'band'}, dimensions={0}, use_global_device_ids=true | all-gather | bytes 655360 | tf_op jit(solution)/shard_map/all_gather | solution.py:138
  24.7 1.0 copy.48
  25.8 1.9 multiply_reduce_fusion.2
  27.6 15.3 %all_gather.18 = bf16[512,512]{1,0:T(8,128)(2,1)S(1)} all-gather(bf16[128,512]{1,0:T(8,128)(2,1)S(1)} %get-tuple-element.82), channel_id=1, replica_groups=mesh['view'=32,'band'=4,'batch'=4] {'band'}, dimensions={0}, use_global_device_ids=true | all-gather | bytes 655360 | tf_op jit(solution)/shard_map/all_gather | solution.py:139
  43.2 2.3 fusion
  47.2 9.3 %all-gather.3.cloned.1.call-done = bf16[768,1536]{1,0:T(8,128)(2,1)} async-done(((bf16[192,1536]{1,0:T(8,128)(2,1)}), bf16[768,1536]{1,0:T(8,128)(2,1)}) %all-gather.3.cloned.1.call-update) | async-done | bytes 2359312 | tf_op jit(solution)/shard_map/all_gather | solution.py:62
  56.6 4.3 %copy.50 = bf16[768,1536]{0,1:T(8,128)(2,1)} copy(bf16[768,1536]{1,0:T(8,128)(2,1)} %all-gather.3.cloned.1.call-done) | data formatting | bytes 4718592 | tf_op jit(solution)/shard_map/all_gather | solution.py:62
  60.8 2.6 fusion.6
  64.1 30.6 %all_to_all.32 = bf16[32,1,16,128]{3,2,1,0:T(8,128)(2,1)S(1)} all-to-all(bf16[32,1,16,128]{3,2,1,0:T(8,128)(2,1)S(1)} %bitcast.147), channel_id=1, replica_groups=mesh['view'=32,'band'=4,'batch'=4] {'view'}, dimensions={0} | all-to-all | bytes 262144 | tf_op jit(solution)/shard_map/all_to_all | solution.py:104
  94.7 19.1 %all_to_all.33 = bf16[32,1,16,128]{3,2,1,0:T(8,128)(2,1)S(1)} all-to-all(bf16[32,1,16,128]{3,2,1,0:T(8,128)(2,1)S(1)} %bitcast.145), channel_id=1, replica_groups=mesh['view'=32,'band'=4,'batch'=4] {'view'}, dimensions={0} | all-to-all | bytes 262144 | tf_op jit(solution)/shard_map/all_to_all | solution.py:103
  113.8 5.1 %all-to-all-start = ((bf16[32,1,16,128]{3,2,1,0:T(8,128)(2,1)}), bf16[32,1,16,128]{3,2,1,0:T(8,128)(2,1)S(1)}, u32[]{:S(2)}, u32[]{:S(2)}) async-start(bf16[32,1,16,128]{3,2,1,0:T(8,128)(2,1)} %bitcast.14), calls=%async_computation | async-start | bytes 262144 | tf_op jit(solution)/shard_map/all_to_all | solution.py:105
  119.2 13.9 %all-to-all-done = bf16[32,1,16,128]{3,2,1,0:T(8,128)(2,1)S(1)} async-done(((bf16[32,1,16,128]{3,2,1,0:T(8,128)(2,1)}), bf16[32,1,16,128]{3,2,1,0:T(8,128)(2,1)S(1)}, u32[]{:S(2)}, u32[]{:S(2)}) %all-to-all-start) | async-done | bytes 131104 | tf_op jit(solution)/shard_map/all_to_all | solution.py:105
  136.2 1.4 reduce.1
  138.3 5.9 %all-to-all-start.3 = ((bf16[32,2,1024]{2,1,0:T(2,128)(2,1)}), bf16[32,2,1024]{2,1,0:T(2,128)(2,1)}, u32[]{:S(2)}, u32[]{:S(2)}) async-start(bf16[32,2,1024]{2,1,0:T(2,128)(2,1)} %reshape.216), calls=%async_computation.3 | async-start | bytes 262144 | tf_op jit(solution)/shard_map/all_to_all | solution.py:57
  144.2 13.5 %all_gather.21 = bf16[512,768]{0,1:T(8,128)(2,1)S(1)} all-gather(bf16[512,192]{0,1:T(8,128)(2,1)} %param.16), channel_id=1, replica_groups=mesh['view'=32,'band'=4,'batch'=4] {'band'}, dimensions={1}, use_global_device_ids=true | all-gather | bytes 983040 | tf_op jit(solution)/shard_map/all_gather | solution.py:74
  157.8 1.2 copy.61
  158.9 4.3 %copy.62 = bf16[768,1536]{0,1:T(8,128)(2,1)} copy(bf16[768,1536]{1,0:T(8,128)(2,1)} %all-gather.5.cloned.1.call-done) | data formatting | bytes 4718592 | tf_op jit(solution)/shard_map/all_gather | solution.py:62
  163.2 1.4 reshape.217
  164.6 1.6 multiply_reduce_fusion.3
  168.1 27.2 %all_to_all.34 = bf16[32,1,16,128]{3,2,1,0:T(8,128)(2,1)S(1)} all-to-all(bf16[32,1,16,128]{3,2,1,0:T(8,128)(2,1)S(1)} %bitcast.148), channel_id=1, replica_groups=mesh['view'=32,'band'=4,'batch'=4] {'view'}, dimensions={0} | all-to-all | bytes 262144 | tf_op jit(solution)/shard_map/all_to_all | solution.py:104
  195.3 18.5 %all_to_all.35 = bf16[32,1,16,128]{3,2,1,0:T(8,128)(2,1)S(1)} all-to-all(bf16[32,1,16,128]{3,2,1,0:T(8,128)(2,1)S(1)} %bitcast.146), channel_id=1, replica_groups=mesh['view'=32,'band'=4,'batch'=4] {'view'}, dimensions={0} | all-to-all | bytes 262144 | tf_op jit(solution)/shard_map/all_to_all | solution.py:103
  213.8 5.2 %all-to-all-start.4 = ((bf16[32,1,16,128]{3,2,1,0:T(8,128)(2,1)}), bf16[32,1,16,128]{3,2,1,0:T(8,128)(2,1)S(1)}, u32[]{:S(2)}, u32[]{:S(2)}) async-start(bf16[32,1,16,128]{3,2,1,0:T(8,128)(2,1)} %bitcast.33), calls=%async_computation.4 | async-start | bytes 262144 | tf_op jit(solution)/shard_map/all_to_all | solution.py:105
  219.7 1.3 copy-done.2
  221.4 11.8 %all-to-all-done.4 = bf16[32,1,16,128]{3,2,1,0:T(8,128)(2,1)S(1)} async-done(((bf16[32,1,16,128]{3,2,1,0:T(8,128)(2,1)}), bf16[32,1,16,128]{3,2,1,0:T(8,128)(2,1)S(1)}, u32[]{:S(2)}, u32[]{:S(2)}) %all-to-all-start.4) | async-done | bytes 131104 | tf_op jit(solution)/shard_map/all_to_all | solution.py:105
  233.4 2.1 fusion.19
  235.7 1.5 reduce.2
  237.8 5.1 %all-to-all-start.7 = ((bf16[32,2,1024]{2,1,0:T(2,128)(2,1)}), bf16[32,2,1024]{2,1,0:T(2,128)(2,1)S(1)}, u32[]{:S(2)}, u32[]{:S(2)}) async-start(bf16[32,2,1024]{2,1,0:T(2,128)(2,1)} %reshape.218), calls=%async_computation.7 | async-start | bytes 262144 | tf_op jit(solution)/shard_map/all_to_all | solution.py:57
  243.0 14.1 %all_gather.23 = bf16[512,768]{0,1:T(8,128)(2,1)} all-gather(bf16[512,192]{0,1:T(8,128)(2,1)S(1)} %copy-done.7), channel_id=1, replica_groups=mesh['view'=32,'band'=4,'batch'=4] {'band'}, dimensions={1}, use_global_device_ids=true | all-gather | bytes 983040 | tf_op jit(solution)/shard_map/all_gather | solution.py:74
  257.0 2.3 copy.73
  259.5 2.1 fusion.10
  (63 shorter events, 13.5 us)
Async XLA Ops:
  6.5 3.7 %copy-start = (bf16[768,1536]{1,0:T(8,128)(2,1)S(1)}, bf16[768,1536]{1,0:T(8,128)(2,1)}, u32[]{:S(2)}) copy-start(bf16[768,1536]{1,0:T(8,128)(2,1)} %param.12) | copy-start | bytes 7077892
  6.5 50.0 %all-gather.3.cloned.1.call-start = ((), (), s32[]{:S(2)}) async-start(), calls=%async_computation.8 | async-start | bytes 2949120 | tf_op jit(solution)/shard_map/all_gather | solution.py:62
  7.3 151.7 %all-gather.5.cloned.1.call-start = ((), (), s32[]{:S(2)}) async-start(), calls=%async_computation.9 | async-start | bytes 2949120 | tf_op jit(solution)/shard_map/all_gather | solution.py:62
  43.2 2.3 copy-start.3
  45.5 0.9 copy-start.4
  45.5 1.2 copy-start.5
  45.5 1.6 copy-start.8
  113.8 19.3 %all-to-all-start = ((bf16[32,1,16,128]{3,2,1,0:T(8,128)(2,1)}), bf16[32,1,16,128]{3,2,1,0:T(8,128)(2,1)S(1)}, u32[]{:S(2)}, u32[]{:S(2)}) async-start(bf16[32,1,16,128]{3,2,1,0:T(8,128)(2,1)} %bitcast.14), calls=%async_computation | async-start | bytes 262144 | tf_op jit(solution)/shard_map/all_to_all | solution.py:105
  134.0 0.9 copy-start.6
  138.3 24.9 %all-to-all-start.3 = ((bf16[32,2,1024]{2,1,0:T(2,128)(2,1)}), bf16[32,2,1024]{2,1,0:T(2,128)(2,1)}, u32[]{:S(2)}, u32[]{:S(2)}) async-start(bf16[32,2,1024]{2,1,0:T(2,128)(2,1)} %reshape.216), calls=%async_computation.3 | async-start | bytes 262144 | tf_op jit(solution)/shard_map/all_to_all | solution.py:57
  163.2 3.1 %copy-start.9 = (f32[768]{0:T(1024)S(1)}, f32[768]{0:T(1024)}, u32[]{:S(2)}) copy-start(f32[768]{0:T(1024)} %param.17) | copy-start | bytes 9220
  164.6 1.9 copy-start.1
  213.8 19.5 %all-to-all-start.4 = ((bf16[32,1,16,128]{3,2,1,0:T(8,128)(2,1)}), bf16[32,1,16,128]{3,2,1,0:T(8,128)(2,1)S(1)}, u32[]{:S(2)}, u32[]{:S(2)}) async-start(bf16[32,1,16,128]{3,2,1,0:T(8,128)(2,1)} %bitcast.33), calls=%async_computation.4 | async-start | bytes 262144 | tf_op jit(solution)/shard_map/all_to_all | solution.py:105
  219.7 1.4 copy-start.2
  233.4 9.6 %copy-start.7 = (bf16[512,192]{0,1:T(8,128)(2,1)S(1)}, bf16[512,192]{0,1:T(8,128)(2,1)}, u32[]{:S(2)}) copy-start(bf16[512,192]{0,1:T(8,128)(2,1)} %param.19) | copy-start | bytes 589828
  237.8 21.5 %all-to-all-start.7 = ((bf16[32,2,1024]{2,1,0:T(2,128)(2,1)}), bf16[32,2,1024]{2,1,0:T(2,128)(2,1)S(1)}, u32[]{:S(2)}, u32[]{:S(2)}) async-start(bf16[32,2,1024]{2,1,0:T(2,128)(2,1)} %reshape.218), calls=%async_computation.7 | async-start | bytes 262144 | tf_op jit(solution)/shard_map/all_to_all | solution.py:57
Sparse Core Ops, SparseCore 0:
  9.4 47.0 all-gather.2
  58.6 41.9 all-gather.4
where the time goes:
time: 269 us; the launch traced here: 268 us
  blocking collectives  152 us (57%)
  waiting for transfers between devices  36.4 us (14%)
  local copies, waits for them, and re-layouts  23.1 us (9%)
  starting transfers between devices  21.3 us (8%)
  matrix products  14 us (5%)
  between operations  13.8 us (5%)
  other arithmetic  8.23 us (3%)
    all_to_all x2, blocking collectives, row_sublayer(): lax.all_to_all(triple[1], 'view', split_axis=0, concat_axis=2, tiled=True)  57.8 us
    all_to_all x2, blocking collectives, row_sublayer(): lax.all_to_all(triple[0], 'view', split_axis=0, concat_axis=2, tiled=True)  37.7 us
    all_gather x2, blocking collectives, mix_parts(): piece = lax.all_gather(shard, 'band', axis=1, tiled=True)  27.6 us
    all_to_all x2, waiting for transfers between devices, row_sublayer(): lax.all_to_all(triple[2], 'view', split_axis=0, concat_axis=2, tiled=True)  25.7 us
    all_gather x1, blocking collectives, local(): values = lax.all_gather(triple[:, 2 * inner:], 'band', axis=0, tiled=True)  15.3 us
    all_gather x1, blocking collectives, local(): lax.all_gather(triple[:, inner:2 * inner], 'band', axis=0, tiled=True)  13.1 us
    all_to_all x2, starting transfers between devices, attend_units(): lax.all_to_all(attended[None], 'view', split_axis=2, concat_axis=0, tiled...  11 us
    all_to_all x2, starting transfers between devices, row_sublayer(): lax.all_to_all(triple[2], 'view', split_axis=0, concat_axis=2, tiled=True)  10.3 us
  transfers between devices with their start and end apart: 6, of which 3 were waited for; matrix products, arithmetic and copies ran while one was open for 12% of the time, Pallas kernels for 0%

commit v1 on v0

--- a/solution.py
+++ b/solution.py
@@ -59,7 +59,9 @@
 
 def project_parts(normed, shard):
     groups = shard.shape[1] // (2 * HEAD_DIM)
-    piece = lax.all_gather(shard, "band", axis=0, tiled=True)
+    piece = jnp.concatenate(
+        lax.all_to_all(jnp.stack([shard] * lax.axis_size("band")), "band", 0, 0), axis=0
+    )
     count = piece.shape[0]
     return jnp.einsum(
         "rcd,dpw->rpcw",

time: 269 us -> 298 us (1.11)
  blocking collectives: 152 us -> 195 us
  between operations: 13.8 us -> 0.38 us
  waiting for transfers between devices: 36.4 us -> 27.5 us
  local copies, waits for them, and re-layouts: 23.1 us -> 29 us
  starting transfers between devices: 21.3 us -> 25.6 us
  other arithmetic: 8.23 us -> 4.39 us
    all_gather x1, blocking collectives: 13.1 us -> 36.8 us  [local(): lax.all_gather(triple[:, inner:2 * inner], 'band', axis=0, tiled=True)]
    all_to_all x0 -> x1, blocking collectives: none -> 18.4 us  [row_sublayer(): lax.all_to_all(triple[2], 'view', split_axis=0, concat_axis=2, tiled=True)]
    all_to_all x0 -> x2, waiting for transfers between devices: none -> 15.6 us  [project_parts(): lax.all_to_all(jnp.stack([shard] * lax.axis_size('band')), 'band', 0, 0)]
    another operation x0 -> x4, local copies, waits for them, and re-layouts: none -> 15.3 us  [the longest x2 10.9 us: project_parts(): piece.reshape(count, groups, 2 * HEAD_DIM)]
    all_to_all x2 -> x1, waiting for transfers between devices: 25.7 us -> 11.8 us  [row_sublayer(): lax.all_to_all(triple[2], 'view', split_axis=0, concat_axis=2, tiled=True)]
    all_gather x2 -> x0, waiting for transfers between devices: 9.32 us -> none  [project_parts(): piece = lax.all_gather(shard, 'band', axis=0, tiled=True)]
    all_to_all x0 -> x2, starting transfers between devices: none -> 9.11 us  [project_parts(): lax.all_to_all(jnp.stack([shard] * lax.axis_size('band')), 'band', 0, 0)]
    all_gather x2 -> x0, local copies, waits for them, and re-layouts: 8.55 us -> none  [project_parts(): piece = lax.all_gather(shard, 'band', axis=0, tiled=True)]
  transfers between devices with their start and end apart: 6 -> 5, of which waited for: 3 -> 2; matrix products, arithmetic and copies ran while one was open for 12% -> 7% of each run, Pallas kernels for 0% -> 0%
where the time goes in v1:
time: 298 us; the launch traced here: 297 us
  blocking collectives  195 us (65%)
  local copies, waits for them, and re-layouts  29 us (10%)
  waiting for transfers between devices  27.5 us (9%)
  starting transfers between devices  25.6 us (9%)
  matrix products  15.1 us (5%)
  other arithmetic  4.39 us (1%)
    all_to_all x2, blocking collectives, row_sublayer(): lax.all_to_all(triple[1], 'view', split_axis=0, concat_axis=2, tiled=True)  59 us
    all_to_all x2, blocking collectives, row_sublayer(): lax.all_to_all(triple[0], 'view', split_axis=0, concat_axis=2, tiled=True)  39.6 us
    all_gather x1, blocking collectives, local(): lax.all_gather(triple[:, inner:2 * inner], 'band', axis=0, tiled=True)  36.8 us
    all_gather x2, blocking collectives, mix_parts(): piece = lax.all_gather(shard, 'band', axis=1, tiled=True)  27.6 us
    all_to_all x1, blocking collectives, row_sublayer(): lax.all_to_all(triple[2], 'view', split_axis=0, concat_axis=2, tiled=True)  18.4 us
    all_to_all x2, waiting for transfers between devices, project_parts(): lax.all_to_all(jnp.stack([shard] * lax.axis_size('band')), 'band', 0, 0)  15.6 us
    all_gather x1, blocking collectives, local(): values = lax.all_gather(triple[:, 2 * inner:], 'band', axis=0, tiled=True)  13.4 us
    all_to_all x1, waiting for transfers between devices, row_sublayer(): lax.all_to_all(triple[2], 'view', split_axis=0, concat_axis=2, tiled=True)  11.8 us
  transfers between devices with their start and end apart: 5, of which 2 were waited for; matrix products, arithmetic and copies ran while one was open for 7% of the time, Pallas kernels for 0%

profile of v1, /device:TPU:8, one launch (start us, length us, event | category | flops | bytes accessed | tf_op | source)
XLA Modules:
  0.0 296.7 jit_solution(15867715329649235236)
XLA Ops:
  0.0 2.8 stack.4
  2.8 4.6 %all-to-all-start = ((bf16[4,192,1536]{2,1,0:T(8,128)(2,1)}), bf16[4,192,1536]{2,1,0:T(8,128)(2,1)}, u32[]{:S(2)}, u32[]{:S(2)}) async-start(bf16[4,192,1536]{2,1,0:T(8,128)(2,1)} %stack.4), calls=%async_computation | async-start | bytes 4718592 | tf_op jit(solution)/shard_map/all_to_all | solution.py:63
  8.3 36.8 %all_gather.13 = bf16[512,512]{1,0:T(8,128)(2,1)S(1)} all-gather(bf16[128,512]{1,0:T(8,128)(2,1)S(1)} %get-tuple-element.74), channel_id=1, replica_groups=mesh['view'=32,'band'=4,'batch'=4] {'band'}, dimensions={0}, use_global_device_ids=true | all-gather | bytes 655360 | tf_op jit(solution)/shard_map/all_gather | solution.py:140
  45.1 13.4 %all_gather.12 = bf16[512,512]{1,0:T(8,128)(2,1)S(1)} all-gather(bf16[128,512]{1,0:T(8,128)(2,1)S(1)} %get-tuple-element.82), channel_id=1, replica_groups=mesh['view'=32,'band'=4,'batch'=4] {'band'}, dimensions={0}, use_global_device_ids=true | all-gather | bytes 655360 | tf_op jit(solution)/shard_map/all_gather | solution.py:141
  60.5 1.7 multiply_reduce_fusion.2
  64.5 5.4 %reshape_reshape.6 = bf16[768,12,128]{2,1,0:T(8,128)(2,1)} reshape(bf16[4,192,1536]{2,1,0:T(8,128)(2,1)} %all-to-all-done) | data formatting | bytes 4718592 | tf_op jit(solution)/shard_map/reshape;reshape | solution.py:69
  70.0 2.5 fusion.21
  72.5 30.9 %all_to_all.40 = bf16[32,1,16,128]{3,2,1,0:T(8,128)(2,1)S(1)} all-to-all(bf16[32,1,16,128]{3,2,1,0:T(8,128)(2,1)S(1)} %bitcast.150), channel_id=1, replica_groups=mesh['view'=32,'band'=4,'batch'=4] {'view'}, dimensions={0} | all-to-all | bytes 262144 | tf_op jit(solution)/shard_map/all_to_all | solution.py:106
  103.4 18.5 %all_to_all.41 = bf16[32,1,16,128]{3,2,1,0:T(8,128)(2,1)S(1)} all-to-all(bf16[32,1,16,128]{3,2,1,0:T(8,128)(2,1)S(1)} %bitcast.148), channel_id=1, replica_groups=mesh['view'=32,'band'=4,'batch'=4] {'view'}, dimensions={0} | all-to-all | bytes 262144 | tf_op jit(solution)/shard_map/all_to_all | solution.py:105
  121.9 18.4 %all_to_all.84 = bf16[32,1,16,128]{3,2,1,0:T(8,128)(2,1)S(1)} all-to-all(bf16[32,1,16,128]{3,2,1,0:T(8,128)(2,1)S(1)} %bitcast.147), channel_id=1, replica_groups=mesh['view'=32,'band'=4,'batch'=4] {'view'}, dimensions={0} | all-to-all | bytes 262144 | tf_op jit(solution)/shard_map/all_to_all | solution.py:107
  140.3 1.6 stack.5
  141.9 4.5 %all-to-all-start.5 = ((bf16[4,192,1536]{2,1,0:T(8,128)(2,1)}), bf16[4,192,1536]{2,1,0:T(8,128)(2,1)}, u32[]{:S(2)}, u32[]{:S(2)}) async-start(bf16[4,192,1536]{2,1,0:T(8,128)(2,1)} %stack.5), calls=%async_computation.5 | async-start | bytes 4718592 | tf_op jit(solution)/shard_map/all_to_all | solution.py:63
  149.6 1.3 reduce.1
  151.6 15.6 %all-to-all-done.5 = bf16[4,192,1536]{2,1,0:T(8,128)(2,1)} async-done(((bf16[4,192,1536]{2,1,0:T(8,128)(2,1)}), bf16[4,192,1536]{2,1,0:T(8,128)(2,1)}, u32[]{:S(2)}, u32[]{:S(2)}) %all-to-all-start.5) | async-done | bytes 2359328 | tf_op jit(solution)/shard_map/all_to_all | solution.py:63
  167.2 5.6 %all-to-all-start.4 = ((bf16[32,2,1024]{2,1,0:T(2,128)(2,1)}), bf16[32,2,1024]{2,1,0:T(2,128)(2,1)}, u32[]{:S(2)}, u32[]{:S(2)}) async-start(bf16[32,2,1024]{2,1,0:T(2,128)(2,1)} %reshape.212), calls=%async_computation.4 | async-start | bytes 262144 | tf_op jit(solution)/shard_map/all_to_all | solution.py:57
  172.9 13.5 %all_gather.14 = bf16[512,768]{0,1:T(8,128)(2,1)S(1)} all-gather(bf16[512,192]{0,1:T(8,128)(2,1)} %param.16), channel_id=1, replica_groups=mesh['view'=32,'band'=4,'batch'=4] {'band'}, dimensions={1}, use_global_device_ids=true | all-gather | bytes 983040 | tf_op jit(solution)/shard_map/all_gather | solution.py:76
  186.4 1.2 copy.58
  187.6 5.4 %reshape_reshape.7 = bf16[768,12,128]{2,1,0:T(8,128)(2,1)} reshape(bf16[4,192,1536]{2,1,0:T(8,128)(2,1)} %all-to-all-done.5) | data formatting | bytes 4718592 | tf_op jit(solution)/shard_map/reshape;reshape | solution.py:69
  193.1 1.4 reshape.213
  194.5 1.5 multiply_reduce_fusion.3
  196.1 2.4 fusion.18
  199.2 28.1 %all_to_all.85 = bf16[32,1,16,128]{3,2,1,0:T(8,128)(2,1)S(1)} all-to-all(bf16[32,1,16,128]{3,2,1,0:T(8,128)(2,1)S(1)} %bitcast.151), channel_id=1, replica_groups=mesh['view'=32,'band'=4,'batch'=4] {'view'}, dimensions={0} | all-to-all | bytes 262144 | tf_op jit(solution)/shard_map/all_to_all | solution.py:106
  227.4 21.1 %all_to_all.86 = bf16[32,1,16,128]{3,2,1,0:T(8,128)(2,1)S(1)} all-to-all(bf16[32,1,16,128]{3,2,1,0:T(8,128)(2,1)S(1)} %bitcast.149), channel_id=1, replica_groups=mesh['view'=32,'band'=4,'batch'=4] {'view'}, dimensions={0} | all-to-all | bytes 262144 | tf_op jit(solution)/shard_map/all_to_all | solution.py:105
  248.5 5.7 %all-to-all-start.6 = ((bf16[32,1,16,128]{3,2,1,0:T(8,128)(2,1)}), bf16[32,1,16,128]{3,2,1,0:T(8,128)(2,1)S(1)}, u32[]{:S(2)}, u32[]{:S(2)}) async-start(bf16[32,1,16,128]{3,2,1,0:T(8,128)(2,1)} %bitcast.31), calls=%async_computation.6 | async-start | bytes 262144 | tf_op jit(solution)/shard_map/all_to_all | solution.py:107
  254.9 1.3 copy-done.1
  256.6 11.8 %all-to-all-done.6 = bf16[32,1,16,128]{3,2,1,0:T(8,128)(2,1)S(1)} async-done(((bf16[32,1,16,128]{3,2,1,0:T(8,128)(2,1)}), bf16[32,1,16,128]{3,2,1,0:T(8,128)(2,1)S(1)}, u32[]{:S(2)}, u32[]{:S(2)}) %all-to-all-start.6) | async-done | bytes 131104 | tf_op jit(solution)/shard_map/all_to_all | solution.py:107
  268.6 2.1 fusion.35
  270.9 1.3 reduce.2
  272.9 5.2 %all-to-all-start.9 = ((bf16[32,2,1024]{2,1,0:T(2,128)(2,1)}), bf16[32,2,1024]{2,1,0:T(2,128)(2,1)S(1)}, u32[]{:S(2)}, u32[]{:S(2)}) async-start(bf16[32,2,1024]{2,1,0:T(2,128)(2,1)} %reshape.214), calls=%async_computation.9 | async-start | bytes 262144 | tf_op jit(solution)/shard_map/all_to_all | solution.py:57
  278.1 14.1 %all_gather.15 = bf16[512,768]{0,1:T(8,128)(2,1)} all-gather(bf16[512,192]{0,1:T(8,128)(2,1)S(1)} %copy-done.7), channel_id=1, replica_groups=mesh['view'=32,'band'=4,'batch'=4] {'band'}, dimensions={1}, use_global_device_ids=true | all-gather | bytes 983040 | tf_op jit(solution)/shard_map/all_gather | solution.py:76
  292.2 2.3 copy.69
  294.7 2.1 fusion.26
  (64 shorter events, 12.1 us)
Async XLA Ops:
  0.0 7.8 %copy-start = (bf16[768,1536]{1,0:T(8,128)(2,1)S(1)}, bf16[768,1536]{1,0:T(8,128)(2,1)}, u32[]{:S(2)}) copy-start(bf16[768,1536]{1,0:T(8,128)(2,1)} %param.12) | copy-start | bytes 7077892
  2.8 4.6 %copy-start.2 = (bf16[1,8,16,768]{3,2,1,0:T(8,128)(2,1)S(1)}, bf16[1,8,16,768]{3,2,1,0:T(8,128)(2,1)}, u32[]{:S(2)}) copy-start(bf16[1,8,16,768]{3,2,1,0:T(8,128)(2,1)} %param.10) | copy-start | bytes 589828
  2.8 4.8 %copy-start.8 = (f32[768]{0:T(1024)S(1)}, f32[768]{0:T(1024)}, u32[]{:S(2)}) copy-start(f32[768]{0:T(1024)} %param.11) | copy-start | bytes 9220
  2.8 61.7 %all-to-all-start = ((bf16[4,192,1536]{2,1,0:T(8,128)(2,1)}), bf16[4,192,1536]{2,1,0:T(8,128)(2,1)}, u32[]{:S(2)}, u32[]{:S(2)}) async-start(bf16[4,192,1536]{2,1,0:T(8,128)(2,1)} %stack.4), calls=%async_computation | async-start | bytes 4718592 | tf_op jit(solution)/shard_map/all_to_all | solution.py:63
  62.7 0.9 copy-start.3
  62.7 1.2 copy-start.4
  62.8 1.6 copy-start.9
  70.0 70.3 %copy-start.5 = (bf16[192,1536]{1,0:T(8,128)(2,1)S(1)}, bf16[192,1536]{1,0:T(8,128)(2,1)}, u32[]{:S(2)}) copy-start(bf16[192,1536]{1,0:T(8,128)(2,1)} %param.18) | copy-start | bytes 1769476
  141.9 25.4 %all-to-all-start.5 = ((bf16[4,192,1536]{2,1,0:T(8,128)(2,1)}), bf16[4,192,1536]{2,1,0:T(8,128)(2,1)}, u32[]{:S(2)}, u32[]{:S(2)}) async-start(bf16[4,192,1536]{2,1,0:T(8,128)(2,1)} %stack.5), calls=%async_computation.5 | async-start | bytes 4718592 | tf_op jit(solution)/shard_map/all_to_all | solution.py:63
  147.5 0.9 copy-start.6
  167.2 25.8 %all-to-all-start.4 = ((bf16[32,2,1024]{2,1,0:T(2,128)(2,1)}), bf16[32,2,1024]{2,1,0:T(2,128)(2,1)}, u32[]{:S(2)}, u32[]{:S(2)}) async-start(bf16[32,2,1024]{2,1,0:T(2,128)(2,1)} %reshape.212), calls=%async_computation.4 | async-start | bytes 262144 | tf_op jit(solution)/shard_map/all_to_all | solution.py:57
  193.1 2.9 copy-start.10
  248.5 20.0 %all-to-all-start.6 = ((bf16[32,1,16,128]{3,2,1,0:T(8,128)(2,1)}), bf16[32,1,16,128]{3,2,1,0:T(8,128)(2,1)S(1)}, u32[]{:S(2)}, u32[]{:S(2)}) async-start(bf16[32,1,16,128]{3,2,1,0:T(8,128)(2,1)} %bitcast.31), calls=%async_computation.6 | async-start | bytes 262144 | tf_op jit(solution)/shard_map/all_to_all | solution.py:107
  254.9 1.4 copy-start.1
  268.6 9.5 %copy-start.7 = (bf16[512,192]{0,1:T(8,128)(2,1)S(1)}, bf16[512,192]{0,1:T(8,128)(2,1)}, u32[]{:S(2)}) copy-start(bf16[512,192]{0,1:T(8,128)(2,1)} %param.19) | copy-start | bytes 589828
  272.9 21.6 %all-to-all-start.9 = ((bf16[32,2,1024]{2,1,0:T(2,128)(2,1)}), bf16[32,2,1024]{2,1,0:T(2,128)(2,1)S(1)}, u32[]{:S(2)}, u32[]{:S(2)}) async-start(bf16[32,2,1024]{2,1,0:T(2,128)(2,1)} %reshape.214), calls=%async_computation.9 | async-start | bytes 262144 | tf_op jit(solution)/shard_map/all_to_all | solution.py:57
